TPU v7x, 128 devices: a whole 4x4x4 slice. The times are simulated.
128 devices in a mesh: row: 8 (over x_lo, z), col: 16 (over x_hi, y, core).
Axes of the slice: x: 4 (x_hi: 2, x_lo: 2; x = x_hi * 2 + x_lo), y: 4, z: 4, core: 2. Of those that a mesh axis runs over, the one named last changes fastest.
Arguments:
- hessian: float32 [18432, 18432], P('row', 'col'), may hold values from -1 to 5, as said below
- right_side: float32 [18432, 512], P('row'), may hold values from -6 to 6
- mask: int32 [18432, 512], P('row'), may hold values 0 or 1
- damping: float32 [1], replicated, may hold values from 0.4 to 1.2
Outputs:
- solution: float32 [18432, 512], P('row')
Inputs may be any that keep to these rules, and one draw needn't show every extreme that they name: hessian is symmetric and positive definite.
All inputs are finite; a program needn't handle non-finite values. No bound on the sum of `mask` on one device may be relied on, other than what follows from the above.
Results may differ from a plain program's by a relative error of at most 0.0001.
Values sent between devices are 32-bit elements; how exact they have to be, the bound alone decides.
A program may use at most 128 MiB of HBM per device.

v0:
```python
import jax
import jax.numpy as jnp
from jax import lax
from jax.sharding import PartitionSpec as P

ITERS = 3
epsilon = 1e-06


def in_one(arrays, axis):
    ends = [0]
    for a in arrays:
        ends.append(ends[-1] + a.size)
    so_far = lax.psum(jnp.concatenate([a.ravel() for a in arrays]), axis)
    return tuple((so_far[b:e].reshape(a.shape) for a, b, e in zip(arrays, ends, ends[1:])))


def from_root(block, axis, source):
    block = jnp.where(lax.axis_index(axis) == source, block, jnp.zeros_like(block))
    return lax.psum(block, axis)


def rows_for(lines, peers):
    spare = -len(lines) % peers
    return jnp.pad(lines, [(0, spare)] + [(0, 0)] * (lines.ndim - 1))


def sum_by_parts(array, axis):
    lines = array.reshape(-1, *array.shape[1:][-1:])
    own = lax.psum_scatter(
        rows_for(lines, lax.axis_size(axis)), axis, scatter_dimension=0, tiled=True
    )
    whole = lax.all_gather(own, axis).reshape(-1, *lines.shape[1:])
    return lax.slice_in_dim(whole, 0, len(lines)).reshape(array.shape)


def column_sums(first, second):
    return jnp.sum(first * second, axis=0)


def both_sums(residual, applied):
    return in_one((column_sums(residual, residual), column_sums(residual, applied)), "row")


def on_device(hessian, right_side, mask, damping):
    mask_float = mask.astype(jnp.float32)
    damping_value = damping[0]
    blocks_ratio = lax.axis_size("col") // lax.axis_size("row")
    block_width = hessian.shape[1]
    col_position = lax.axis_index("col")

    def masked_apply(vector):
        own_slice = lax.dynamic_slice_in_dim(
            vector, col_position % blocks_ratio * block_width, block_width, 0
        )
        column_block = from_root(own_slice, "row", col_position // blocks_ratio)
        partial_value = jnp.dot(
            hessian,
            column_block,
            precision=lax.Precision.HIGHEST,
            preferred_element_type=jnp.float32,
        )
        summed = sum_by_parts(partial_value, "col")
        return mask_float * (summed + damping_value * vector)

    residual = mask_float * right_side
    direction = residual
    solution = jnp.zeros_like(right_side)
    applied = masked_apply(residual)
    norm_now, inner = both_sums(residual, applied)
    step_size = norm_now / (inner + epsilon)
    along = applied
    for iteration in range(ITERS):
        solution = solution + step_size * direction
        residual = residual - step_size * along
        if iteration + 1 < ITERS:
            applied = masked_apply(residual)
            norm_next, inner = both_sums(residual, applied)
            factor = norm_next / (norm_now + epsilon)
            curvature = inner - factor * norm_next / step_size
            step_size = norm_next / (curvature + epsilon)
            direction = residual + factor * direction
            along = applied + factor * along
            norm_now = norm_next
    return solution


def solution(mesh):
    in_specs = (P("row", "col"), P("row", None), P("row", None), P())
    out_specs = P("row", None)
    return jax.shard_map(
        on_device, mesh=mesh, in_specs=in_specs, out_specs=out_specs, check_vma=False
    )
```

profile of v0, /device:TPU:0, one launch (start us, length us, event | category | flops | bytes accessed | tf_op | source)
XLA Modules:
  0.0 936.5 jit_solution(12849361006295928117)
XLA Ops:
  6.5 4.9 convert_multiply_fusion
  11.5 2.2 copy-done
  13.7 1.7 dynamic-slice_select_fusion.2
  15.4 86.8 %all-reduce.4.cloned.1.call-done = f32[1152,512]{1,0:T(8,128)} async-done(((f32[1152,512]{1,0:T(8,128)}), f32[1152,512]{1,0:T(8,128)}) %all-reduce.4.cloned.1.call-update) | async-done | bytes 2359312 | tf_op jit(solution)/shard_map/psum | solution.py:20
  102.2 37.5 %convolution_bitcast_fusion.2 = f32[2304,512]{0,1:T(8,128)} fusion(f32[1152,512]{1,0:T(8,128)} %all-reduce.4.cloned.1.call-done, f32[2304,1152]{1,0:T(8,128)} %param.4), kind=kOutput, calls=%fused_computation.2 | convolution fusion | flops 16307453952 | bytes 17694720 | tf_op jit(solution)/shard_map/dot_general | solution.py:57
  139.7 6.1 copy.11
  145.9 82.9 %reduce-scatter.10.cloned.1.call-done = f32[144,512]{1,0:T(8,128)} async-done(((f32[2304,512]{1,0:T(8,128)}), f32[144,512]{1,0:T(8,128)}) %reduce-scatter.10.cloned.1.call-update) | async-done | bytes 294928 | tf_op jit(solution)/shard_map/reduce_scatter | solution.py:30
  229.7 58.0 %all-gather.7.cloned.1.call-done = f32[2304,512]{1,0:T(8,128)} async-done(((f32[144,512]{1,0:T(8,128)}), f32[2304,512]{1,0:T(8,128)}) %all-gather.7.cloned.1.call-update) | async-done | bytes 4718608 | tf_op jit(solution)/shard_map/all_gather | solution.py:33
  287.8 6.9 multiply_reduce_fusion.5
  294.7 18.9 %psum.43 = f32[1024]{0:T(1024)S(1)} all-reduce(f32[1024]{0:T(1024)S(1)} %pad_maximum_fusion), channel_id=1, replica_groups=mesh['row'=8,'col'=16] {'row'}, use_global_device_ids=true, to_apply=%region_4.5 | all-reduce | flops 1024 | bytes 8192 | tf_op jit(solution)/shard_map/psum | solution.py:14
  313.6 6.9 multiply_subtract_fusion.1
  320.6 2.1 copy-done.1
  322.7 1.7 dynamic-slice_select_fusion.1
  324.4 80.6 %all-reduce.6.cloned.1.call-done = f32[1152,512]{1,0:T(8,128)} async-done(((f32[1152,512]{1,0:T(8,128)}), f32[1152,512]{1,0:T(8,128)}) %all-reduce.6.cloned.1.call-update) | async-done | bytes 2359312 | tf_op jit(solution)/shard_map/psum | solution.py:20
  405.0 37.5 %convolution_bitcast_fusion.1 = f32[2304,512]{0,1:T(8,128)} fusion(f32[1152,512]{1,0:T(8,128)} %all-reduce.6.cloned.1.call-done, f32[2304,1152]{1,0:T(8,128)} %param.4), kind=kOutput, calls=%fused_computation.1 | convolution fusion | flops 16307453952 | bytes 17694720 | tf_op jit(solution)/shard_map/dot_general | solution.py:57
  442.5 6.1 copy.13
  448.6 83.0 %reduce-scatter.12.cloned.1.call-done = f32[144,512]{1,0:T(8,128)} async-done(((f32[2304,512]{1,0:T(8,128)}), f32[144,512]{1,0:T(8,128)}) %reduce-scatter.12.cloned.1.call-update) | async-done | bytes 294928 | tf_op jit(solution)/shard_map/reduce_scatter | solution.py:30
  531.9 58.1 %all-gather.9.cloned.1.call-done = f32[2304,512]{1,0:T(8,128)} async-done(((f32[144,512]{1,0:T(8,128)}), f32[2304,512]{1,0:T(8,128)}) %all-gather.9.cloned.1.call-update) | async-done | bytes 4718608 | tf_op jit(solution)/shard_map/all_gather | solution.py:33
  590.0 6.9 multiply_reduce_fusion.3
  596.9 18.9 %psum.45 = f32[1024]{0:T(1024)S(1)} all-reduce(f32[1024]{0:T(1024)S(1)} %pad_maximum_fusion.1), channel_id=1, replica_groups=mesh['row'=8,'col'=16] {'row'}, use_global_device_ids=true, to_apply=%region_9.10 | all-reduce | flops 1024 | bytes 8192 | tf_op jit(solution)/shard_map/psum | solution.py:14
  615.9 8.7 multiply_subtract_fusion
  624.6 2.2 copy-done.2
  626.7 1.7 dynamic-slice_select_fusion
  628.4 80.6 %all-reduce.8.cloned.1.call-done = f32[1152,512]{1,0:T(8,128)} async-done(((f32[1152,512]{1,0:T(8,128)}), f32[1152,512]{1,0:T(8,128)}) %all-reduce.8.cloned.1.call-update) | async-done | bytes 2359312 | tf_op jit(solution)/shard_map/psum | solution.py:20
  709.0 37.5 %convolution_bitcast_fusion = f32[2304,512]{0,1:T(8,128)} fusion(f32[1152,512]{1,0:T(8,128)} %all-reduce.8.cloned.1.call-done, f32[2304,1152]{1,0:T(8,128)} %param.4), kind=kOutput, calls=%fused_computation | convolution fusion | flops 16307453952 | bytes 17694720 | tf_op jit(solution)/shard_map/dot_general | solution.py:57
  746.5 6.1 copy.15
  752.6 0.3 all-gather.11.cloned.1.call-start
  752.9 82.7 %reduce-scatter.14.cloned.1.call-done = f32[144,512]{1,0:T(8,128)} async-done(((f32[2304,512]{1,0:T(8,128)}), f32[144,512]{1,0:T(8,128)}) %reduce-scatter.14.cloned.1.call-update) | async-done | bytes 294928 | tf_op jit(solution)/shard_map/reduce_scatter | solution.py:30
  835.6 58.9 %all-gather.11.cloned.1.call-done = f32[2304,512]{1,0:T(8,128)} async-done(((f32[144,512]{1,0:T(8,128)}), f32[2304,512]{1,0:T(8,128)}) %all-gather.11.cloned.1.call-update) | async-done | bytes 4718608 | tf_op jit(solution)/shard_map/all_gather | solution.py:33
  894.5 6.9 multiply_reduce_fusion.1
  901.5 18.9 %psum.47 = f32[1024]{0:T(1024)S(1)} all-reduce(f32[1024]{0:T(1024)S(1)} %pad_maximum_fusion.2), channel_id=1, replica_groups=mesh['row'=8,'col'=16] {'row'}, use_global_device_ids=true, to_apply=%region_14.15 | all-reduce | flops 1024 | bytes 8192 | tf_op jit(solution)/shard_map/psum | solution.py:14
  920.4 9.2 multiply_add_fusion
  (26 shorter events, 0.9 us)
Async XLA Ops:
  6.5 95.7 %all-reduce.4.cloned.1.call-start = ((), (), s32[]{:S(2)}) async-start(), calls=%async_computation.3 | async-start | bytes 4718592 | tf_op jit(solution)/shard_map/psum | solution.py:20
  11.5 2.2 copy-start
  15.4 213.5 %reduce-scatter.10.cloned.1.call-start = ((), (), s32[]{:S(2)}) async-start(), calls=%async_computation.9 | async-start | bytes 5013504 | tf_op jit(solution)/shard_map/reduce_scatter | solution.py:30
  145.9 141.9 %all-gather.7.cloned.1.call-start = ((), (), s32[]{:S(2)}) async-start(), calls=%async_computation.6 | async-start | bytes 5013504 | tf_op jit(solution)/shard_map/all_gather | solution.py:33
  228.9 176.1 %all-reduce.6.cloned.1.call-start = ((), (), s32[]{:S(2)}) async-start(), calls=%async_computation.4 | async-start | bytes 4718592 | tf_op jit(solution)/shard_map/psum | solution.py:20
  320.5 2.1 copy-start.1
  324.4 207.2 %reduce-scatter.12.cloned.1.call-start = ((), (), s32[]{:S(2)}) async-start(), calls=%async_computation.10 | async-start | bytes 5013504 | tf_op jit(solution)/shard_map/reduce_scatter | solution.py:30
  448.6 141.4 %all-gather.9.cloned.1.call-start = ((), (), s32[]{:S(2)}) async-start(), calls=%async_computation.7 | async-start | bytes 5013504 | tf_op jit(solution)/shard_map/all_gather | solution.py:33
  531.6 177.4 %all-reduce.8.cloned.1.call-start = ((), (), s32[]{:S(2)}) async-start(), calls=%async_computation.5 | async-start | bytes 4718592 | tf_op jit(solution)/shard_map/psum | solution.py:20
  624.5 2.2 copy-start.2
  628.4 207.2 %reduce-scatter.14.cloned.1.call-start = ((), (), s32[]{:S(2)}) async-start(), calls=%async_computation.11 | async-start | bytes 5013504 | tf_op jit(solution)/shard_map/reduce_scatter | solution.py:30
  752.6 141.9 %all-gather.11.cloned.1.call-start = ((), (), s32[]{:S(2)}) async-start(), calls=%async_computation.8 | async-start | bytes 5013504 | tf_op jit(solution)/shard_map/all_gather | solution.py:33
Sparse Core Ops, SparseCore 0:
  15.5 86.6 all-reduce.3
  146.0 82.7 reduce-scatter.9
  231.6 56.1 all-gather.6
  324.5 80.4 all-reduce.5
  448.7 82.8 reduce-scatter.11
  533.9 56.0 all-gather.8
  628.5 80.4 all-reduce.7
  752.7 82.8 reduce-scatter.13
  838.4 56.0 all-gather.10
where the time goes:
time: 946 us; the launch traced here: 937 us
  waiting for transfers between devices  672 us (71%)
  matrix products  112 us (12%)
  blocking collectives  56.7 us (6%)
  other arithmetic  55.5 us (6%)
  local copies, waits for them, and re-layouts  24.8 us (3%)
  between operations  14.3 us (2%)
    reduce_scatter x3, waiting for transfers between devices, sum_by_parts(): lax.psum_scatter(rows_for(lines, lax.axis_size(axis)), axis, scatter_dime...  249 us
    psum x3, waiting for transfers between devices, from_root(): return lax.psum(block, axis)  248 us
    all_gather x3, waiting for transfers between devices, sum_by_parts(): whole = lax.all_gather(own, axis).reshape(-1, *lines.shape[1:])  175 us
    dot_general x3, matrix products, masked_apply(): jnp.dot(hessian, column_block, precision=lax.Precision.HIGHEST, preferred...  112 us
    psum x3, blocking collectives, in_one(): so_far = lax.psum(jnp.concatenate([a.ravel() for a in arrays]), axis)  56.7 us
    unnamed x9, local copies, waits for them, and re-layouts  24.8 us
    reduce_sum x3, other arithmetic, column_sums(): return jnp.sum(first * second, axis=0)  20.8 us
  transfers between devices with their start and end apart: 9, of which 9 were waited for; matrix products, arithmetic and copies ran while one was open for 0% of the time, Pallas kernels for 0%

commit v1 on v0

--- a/solution.py
+++ b/solution.py
@@ -11,7 +11,9 @@
     ends = [0]
     for a in arrays:
         ends.append(ends[-1] + a.size)
-    so_far = lax.psum(jnp.concatenate([a.ravel() for a in arrays]), axis)
+    own_2 = jnp.concatenate([a.ravel() for a in arrays])
+    parts = lax.all_gather(own_2, axis)
+    so_far = jnp.sum(parts, axis=0)
     return tuple((so_far[b:e].reshape(a.shape) for a, b, e in zip(arrays, ends, ends[1:])))
 
 

time: 946 us -> 977 us (1.033)
  blocking collectives: 56.7 us -> 84.2 us
    all_gather x0 -> x3, blocking collectives: none -> 84.2 us  [in_one(): parts = lax.all_gather(own_2, axis)]
    psum x3 -> x0, blocking collectives: 56.7 us -> none  [in_one(): so_far = lax.psum(jnp.concatenate([a.ravel() for a in arrays]), axis)]
where the time goes in v1:
time: 977 us; the launch traced here: 967 us
  waiting for transfers between devices  675 us (69%)
  matrix products  112 us (11%)
  blocking collectives  84.2 us (9%)
  other arithmetic  55.6 us (6%)
  local copies, waits for them, and re-layouts  24.8 us (3%)
  between operations  14.4 us (1%)
    psum x3, waiting for transfers between devices, from_root(): return lax.psum(block, axis)  251 us
    reduce_scatter x3, waiting for transfers between devices, sum_by_parts(): lax.psum_scatter(rows_for(lines, lax.axis_size(axis)), axis, scatter_dime...  249 us
    all_gather x3, waiting for transfers between devices, sum_by_parts(): whole = lax.all_gather(own, axis).reshape(-1, *lines.shape[1:])  175 us
    dot_general x3, matrix products, masked_apply(): jnp.dot(hessian, column_block, precision=lax.Precision.HIGHEST, preferred...  112 us
    all_gather x3, blocking collectives, in_one(): parts = lax.all_gather(own_2, axis)  84.2 us
    unnamed x9, local copies, waits for them, and re-layouts  24.8 us
    reduce_sum x3, other arithmetic, column_sums(): return jnp.sum(first * second, axis=0)  20.8 us
  transfers between devices with their start and end apart: 9, of which 9 were waited for; matrix products, arithmetic and copies ran while one was open for 0% of the time, Pallas kernels for 0%

profile of v1, /device:TPU:0, one launch (start us, length us, event | category | flops | bytes accessed | tf_op | source)
XLA Modules:
  0.0 967.0 jit_solution(11126204946080373285)
XLA Ops:
  6.5 4.9 convert_multiply_fusion
  11.5 2.2 copy-done
  13.7 1.7 dynamic-slice_select_fusion.2
  15.4 86.8 %all-reduce.4.cloned.1.call-done = f32[1152,512]{1,0:T(8,128)} async-done(((f32[1152,512]{1,0:T(8,128)}), f32[1152,512]{1,0:T(8,128)}) %all-reduce.4.cloned.1.call-update) | async-done | bytes 2359312 | tf_op jit(solution)/shard_map/psum | solution.py:22
  102.2 37.5 %convolution_bitcast_fusion.2 = f32[2304,512]{0,1:T(8,128)} fusion(f32[1152,512]{1,0:T(8,128)} %all-reduce.4.cloned.1.call-done, f32[2304,1152]{1,0:T(8,128)} %param.4), kind=kOutput, calls=%fused_computation.2 | convolution fusion | flops 16307453952 | bytes 17694720 | tf_op jit(solution)/shard_map/dot_general | solution.py:59
  139.7 6.1 copy.14
  145.9 82.9 %reduce-scatter.10.cloned.1.call-done = f32[144,512]{1,0:T(8,128)} async-done(((f32[2304,512]{1,0:T(8,128)}), f32[144,512]{1,0:T(8,128)}) %reduce-scatter.10.cloned.1.call-update) | async-done | bytes 294928 | tf_op jit(solution)/shard_map/reduce_scatter | solution.py:32
  229.7 58.0 %all-gather.10.cloned.1.call-done = f32[2304,512]{1,0:T(8,128)} async-done(((f32[144,512]{1,0:T(8,128)}), f32[2304,512]{1,0:T(8,128)}) %all-gather.10.cloned.1.call-update) | async-done | bytes 4718608 | tf_op jit(solution)/shard_map/all_gather | solution.py:35
  287.8 6.9 multiply_reduce_fusion.5
  294.7 28.1 %all-gather.1 = f32[8192]{0:T(1024)S(1)} all-gather(f32[1024]{0:T(1024)S(1)} %pad_maximum_fusion), channel_id=3, replica_groups=mesh['row'=8,'col'=16] {'row'}, dimensions={0}, use_global_device_ids=true | all-gather | bytes 36864 | tf_op jit(solution)/shard_map/all_gather | solution.py:15
  322.8 6.9 multiply_subtract_fusion.1
  329.8 2.1 copy-done.1
  331.9 1.7 dynamic-slice_select_fusion.1
  333.6 82.1 %all-reduce.6.cloned.1.call-done = f32[1152,512]{1,0:T(8,128)} async-done(((f32[1152,512]{1,0:T(8,128)}), f32[1152,512]{1,0:T(8,128)}) %all-reduce.6.cloned.1.call-update) | async-done | bytes 2359312 | tf_op jit(solution)/shard_map/psum | solution.py:22
  415.7 37.5 %convolution_bitcast_fusion.1 = f32[2304,512]{0,1:T(8,128)} fusion(f32[1152,512]{1,0:T(8,128)} %all-reduce.6.cloned.1.call-done, f32[2304,1152]{1,0:T(8,128)} %param.4), kind=kOutput, calls=%fused_computation.1 | convolution fusion | flops 16307453952 | bytes 17694720 | tf_op jit(solution)/shard_map/dot_general | solution.py:59
  453.1 6.1 copy.16
  459.3 83.0 %reduce-scatter.12.cloned.1.call-done = f32[144,512]{1,0:T(8,128)} async-done(((f32[2304,512]{1,0:T(8,128)}), f32[144,512]{1,0:T(8,128)}) %reduce-scatter.12.cloned.1.call-update) | async-done | bytes 294928 | tf_op jit(solution)/shard_map/reduce_scatter | solution.py:32
  542.5 58.1 %all-gather.12.cloned.1.call-done = f32[2304,512]{1,0:T(8,128)} async-done(((f32[144,512]{1,0:T(8,128)}), f32[2304,512]{1,0:T(8,128)}) %all-gather.12.cloned.1.call-update) | async-done | bytes 4718608 | tf_op jit(solution)/shard_map/all_gather | solution.py:35
  600.6 6.9 multiply_reduce_fusion.3
  607.6 28.1 %all-gather.3 = f32[8192]{0:T(1024)S(1)} all-gather(f32[1024]{0:T(1024)S(1)} %pad_maximum_fusion.1), channel_id=5, replica_groups=mesh['row'=8,'col'=16] {'row'}, dimensions={0}, use_global_device_ids=true | all-gather | bytes 36864 | tf_op jit(solution)/shard_map/all_gather | solution.py:15
  635.7 8.7 multiply_subtract_fusion
  644.4 2.2 copy-done.2
  646.6 1.7 dynamic-slice_select_fusion
  648.3 82.1 %all-reduce.8.cloned.1.call-done = f32[1152,512]{1,0:T(8,128)} async-done(((f32[1152,512]{1,0:T(8,128)}), f32[1152,512]{1,0:T(8,128)}) %all-reduce.8.cloned.1.call-update) | async-done | bytes 2359312 | tf_op jit(solution)/shard_map/psum | solution.py:22
  730.4 37.5 %convolution_bitcast_fusion = f32[2304,512]{0,1:T(8,128)} fusion(f32[1152,512]{1,0:T(8,128)} %all-reduce.8.cloned.1.call-done, f32[2304,1152]{1,0:T(8,128)} %param.4), kind=kOutput, calls=%fused_computation | convolution fusion | flops 16307453952 | bytes 17694720 | tf_op jit(solution)/shard_map/dot_general | solution.py:59
  767.8 6.1 copy.18
  773.9 0.3 all-gather.14.cloned.1.call-start
  774.2 82.7 %reduce-scatter.14.cloned.1.call-done = f32[144,512]{1,0:T(8,128)} async-done(((f32[2304,512]{1,0:T(8,128)}), f32[144,512]{1,0:T(8,128)}) %reduce-scatter.14.cloned.1.call-update) | async-done | bytes 294928 | tf_op jit(solution)/shard_map/reduce_scatter | solution.py:32
  856.9 58.9 %all-gather.14.cloned.1.call-done = f32[2304,512]{1,0:T(8,128)} async-done(((f32[144,512]{1,0:T(8,128)}), f32[2304,512]{1,0:T(8,128)}) %all-gather.14.cloned.1.call-update) | async-done | bytes 4718608 | tf_op jit(solution)/shard_map/all_gather | solution.py:35
  915.8 6.9 multiply_reduce_fusion.1
  922.8 28.1 %all-gather.5 = f32[8192]{0:T(1024)S(1)} all-gather(f32[1024]{0:T(1024)S(1)} %pad_maximum_fusion.2), channel_id=7, replica_groups=mesh['row'=8,'col'=16] {'row'}, dimensions={0}, use_global_device_ids=true | all-gather | bytes 36864 | tf_op jit(solution)/shard_map/all_gather | solution.py:15
  950.9 9.2 multiply_add_fusion
  (32 shorter events, 1.0 us)
Async XLA Ops:
  6.5 95.7 %all-reduce.4.cloned.1.call-start = ((), (), s32[]{:S(2)}) async-start(), calls=%async_computation.3 | async-start | bytes 4718592 | tf_op jit(solution)/shard_map/psum | solution.py:22
  11.5 2.2 copy-start
  15.4 213.5 %reduce-scatter.10.cloned.1.call-start = ((), (), s32[]{:S(2)}) async-start(), calls=%async_computation.9 | async-start | bytes 5013504 | tf_op jit(solution)/shard_map/reduce_scatter | solution.py:32
  145.9 141.9 %all-gather.10.cloned.1.call-start = ((), (), s32[]{:S(2)}) async-start(), calls=%async_computation.6 | async-start | bytes 5013504 | tf_op jit(solution)/shard_map/all_gather | solution.py:35
  228.9 186.8 %all-reduce.6.cloned.1.call-start = ((), (), s32[]{:S(2)}) async-start(), calls=%async_computation.4 | async-start | bytes 4718592 | tf_op jit(solution)/shard_map/psum | solution.py:22
  329.7 2.1 copy-start.1
  333.5 208.7 %reduce-scatter.12.cloned.1.call-start = ((), (), s32[]{:S(2)}) async-start(), calls=%async_computation.10 | async-start | bytes 5013504 | tf_op jit(solution)/shard_map/reduce_scatter | solution.py:32
  459.2 141.4 %all-gather.12.cloned.1.call-start = ((), (), s32[]{:S(2)}) async-start(), calls=%async_computation.7 | async-start | bytes 5013504 | tf_op jit(solution)/shard_map/all_gather | solution.py:35
  542.3 188.1 %all-reduce.8.cloned.1.call-start = ((), (), s32[]{:S(2)}) async-start(), calls=%async_computation.5 | async-start | bytes 4718592 | tf_op jit(solution)/shard_map/psum | solution.py:22
  644.4 2.2 copy-start.2
  648.2 208.7 %reduce-scatter.14.cloned.1.call-start = ((), (), s32[]{:S(2)}) async-start(), calls=%async_computation.11 | async-start | bytes 5013504 | tf_op jit(solution)/shard_map/reduce_scatter | solution.py:32
  773.9 141.9 %all-gather.14.cloned.1.call-start = ((), (), s32[]{:S(2)}) async-start(), calls=%async_computation.8 | async-start | bytes 5013504 | tf_op jit(solution)/shard_map/all_gather | solution.py:35
Sparse Core Ops, SparseCore 0:
  15.5 86.6 all-reduce.3
  146.0 82.7 reduce-scatter.9
  231.6 56.1 all-gather.9
  333.7 81.9 all-reduce.5
  459.4 82.8 reduce-scatter.11
  544.6 56.0 all-gather.11
  648.4 81.9 all-reduce.7
  774.1 82.8 reduce-scatter.13
  859.7 56.0 all-gather.13
